TPU v7x, 256 devices: a whole 4x4x8 slice. The times are simulated.
256 devices in a mesh: group: 16 (over y, x), member: 16 (over z, core).
Axes of the slice: x: 4, y: 4, z: 8, core: 2. Of those that a mesh axis runs over, the one named last changes fastest.
Arguments:
- features: bfloat16 [262144, 1024], P(('group', 'member')), may hold values from -6 to 6
- w_self: bfloat16 [1024, 1024], replicated, may hold values from -0.1875 to 0.1875
- w_neigh: bfloat16 [1024, 1024], replicated, may hold values from -0.1875 to 0.1875
- bias: bfloat16 [1024], replicated, may hold values from -3 to 3
- hub_rows: int32 [1536], P(('group', 'member')), may hold values from 0 to 1023
- hub_nbrs: int32 [262144, 8], P(('group', 'member')), may hold values from 0 to 1535
- local_nbrs: int32 [262144, 16], P(('group', 'member')), may hold values from 0 to 1023
- halo_nbrs: int32 [262144, 16], P(('group', 'member')), may hold values from 0 to 2047
- degrees: int32 [3, 262144], P(None, ('group', 'member')), may hold values from 0 to 16, as said below
- send_rows: int32 [256, 16, 128], P(('group', 'member')), may hold values from 0 to 1023
Outputs:
- hidden_out: bfloat16 [262144, 1024], P(('group', 'member'))
Inputs may be any that keep to these rules, and one draw needn't show every extreme that they name: degrees[0] is at least 1 and reaches 16; degrees[1] reaches 8; degrees[2] reaches 16, each in every draw.
All inputs are finite; a program needn't handle non-finite values.
Results may differ from a plain program's by a relative error of at most 0.002.
Values may be sent and summed in bfloat16 or wider, within the bound.
A program may use at most 128 MiB of HBM per device.

v0:
```python
import math
import jax
import jax.numpy as jnp
from jax import lax
from jax.sharding import PartitionSpec as P


def count_table(index_list, valid_mask, total):
    numbers = jnp.arange(total, dtype=jnp.int32)
    tallies = jnp.zeros((index_list.shape[0], total), jnp.float32)
    for slot in range(index_list.shape[1]):
        hits = (index_list[:, slot][:, None] == numbers[None, :]) & valid_mask[:, slot][:, None]
        tallies = tallies + hits.astype(jnp.float32)
    return tallies.astype(jnp.bfloat16)


def block_mean(
    self_features,
    hub_lookup_matrix,
    neighbour_positions,
    local_index_list,
    hub_index_list,
    halo_index_list,
    deg,
):
    klocal = local_index_list.shape[1]
    khub = hub_index_list.shape[1]
    khalo = halo_index_list.shape[1]
    local_valid_mask = jnp.arange(klocal)[None, :] < deg[0][:, None]
    hub_valid_mask = jnp.arange(khub)[None, :] < deg[1][:, None]
    halo_valid_mask = jnp.arange(khalo)[None, :] < deg[2][:, None]
    local_counts = count_table(local_index_list, local_valid_mask, self_features.shape[0])
    neighbour_sum = jnp.dot(local_counts, self_features, preferred_element_type=jnp.float32)
    hub_counts = count_table(hub_index_list, hub_valid_mask, hub_lookup_matrix.shape[0])
    neighbour_sum = neighbour_sum + jnp.dot(
        hub_counts, hub_lookup_matrix, preferred_element_type=jnp.float32
    )
    halo_counts = count_table(halo_index_list, halo_valid_mask, neighbour_positions.shape[0])
    neighbour_sum = neighbour_sum + jnp.dot(
        halo_counts, neighbour_positions, preferred_element_type=jnp.float32
    )
    count = (
        jnp.sum(local_valid_mask.astype(jnp.float32), axis=1)
        + jnp.sum(hub_valid_mask.astype(jnp.float32), axis=1)
        + jnp.sum(halo_valid_mask.astype(jnp.float32), axis=1)
    )
    return (neighbour_sum / count[:, None]).astype(jnp.bfloat16)


def per_device(
    features, w_self, w_neigh, bias, hub_rows, hub_nbrs, local_nbrs, halo_nbrs, degrees, send_rows
):
    rows_here = features.shape[0]
    width = features.shape[1]
    peers = send_rows.shape[1]
    caps = send_rows.shape[2]
    mine = jnp.take(features, hub_rows, axis=0)
    hub_lookup_matrix = lax.all_gather(mine, ("group", "member"), axis=0, tiled=True)
    outgoing = jnp.take(features, send_rows.reshape(peers * caps), axis=0).reshape(
        peers, caps, width
    )
    received = lax.all_to_all(outgoing, "member", split_axis=0, concat_axis=0, tiled=True)
    neighbour_positions = received.reshape(peers * caps, width)
    blk = math.gcd(rows_here, 256)
    nblocks = rows_here // blk
    local_index_list = local_nbrs.reshape(nblocks, blk, local_nbrs.shape[1])
    hub_index_list = hub_nbrs.reshape(nblocks, blk, hub_nbrs.shape[1])
    halo_index_list = halo_nbrs.reshape(nblocks, blk, halo_nbrs.shape[1])
    deg = degrees.reshape(3, nblocks, blk).transpose(1, 0, 2)

    def one(item):
        return block_mean(
            features, hub_lookup_matrix, neighbour_positions, item[0], item[1], item[2], item[3]
        )

    neigh_mean = lax.map(one, (local_index_list, hub_index_list, halo_index_list, deg)).reshape(
        rows_here, width
    )
    value = jnp.dot(features, w_self, preferred_element_type=jnp.float32)
    value = value + jnp.dot(neigh_mean, w_neigh, preferred_element_type=jnp.float32)
    value = value + bias.astype(jnp.float32)[None, :]
    return jnp.maximum(value, 0.0).astype(jnp.bfloat16)


def solution(mesh):
    in_specs = (
        P(("group", "member"), None),
        P(),
        P(),
        P(),
        P(("group", "member")),
        P(("group", "member"), None),
        P(("group", "member"), None),
        P(("group", "member"), None),
        P(None, ("group", "member")),
        P(("group", "member"), None, None),
    )
    out_specs = P(("group", "member"), None)
    return jax.shard_map(
        per_device, mesh=mesh, in_specs=in_specs, out_specs=out_specs, check_vma=False
    )
```

profile of v0, /device:TPU:1, one launch (start us, length us, event | category | flops | bytes accessed | tf_op | source)
XLA Modules:
  0.0 296.7 jit_solution(11345397366022526329)
XLA Ops:
  6.5 0.9 compare_and_fusion
  7.4 0.7 compare_select_fusion
  8.1 12.9 %gather_fusion.1 = bf16[2048,1024]{1,0:T(8,128)(2,1)} fusion(bf16[1024,1024]{1,0:T(8,128)(2,1)} %param.12, s32[2048]{0:T(1024)S(1)} %broadcast_clamp_fusion), kind=kCustom, calls=%fused_computation.1 | custom fusion | bytes 8396800 | tf_op jit(solution)/shard_map/jit(_take)/gather | solution.py:59
  21.0 3.8 %broadcast_select_fusion = bf16[16,128,1024]{2,1,0:T(8,128)(2,1)} fusion(bf16[16,128,1024]{2,1,0:T(8,128)(2,1)} %bitcast.181, pred[16,128]{1,0:T(8,128)(4,1)S(1)} %compare_and_fusion), kind=kLoop, calls=%fused_computation.229 | loop fusion | flops 2097152 | bytes 8390656 | tf_op jit(solution)/shard_map/jit(_take)/select_n | solution.py:59
  24.8 10.1 %all-to-all-start = ((bf16[16,128,1024]{2,1,0:T(8,128)(2,1)}), bf16[16,128,1024]{2,1,0:T(8,128)(2,1)}, u32[]{:S(2)}, u32[]{:S(2)}) async-start(bf16[16,128,1024]{2,1,0:T(8,128)(2,1)} %broadcast_select_fusion), calls=%async_computation | async-start | bytes 8388608 | tf_op jit(solution)/shard_map/all_to_all | solution.py:62
  35.0 2.4 gather_fusion
  37.5 0.7 select_bitcast_fusion
  38.3 5.9 %fusion.130 = f32[1024,1024]{1,0:T(8,128)} fusion(bf16[1024,1024]{1,0:T(8,128)(2,1)} %param.12, bf16[1024,1024]{1,0:T(8,128)(2,1)S(1)} %copy-done), kind=kOutput, calls=%fused_computation.241 | convolution fusion | flops 2147483648 | bytes 8388608 | tf_op jit(solution)/shard_map/dot_general | solution.py:79
  44.2 141.6 %all-gather.3.cloned.1.call-done = bf16[256,6,1024]{2,1,0:T(8,128)(2,1)} async-done(((bf16[1,6,1024]{2,1,0:T(8,128)(2,1)}), bf16[256,6,1024]{2,1,0:T(8,128)(2,1)}) %all-gather.3.cloned.1.call-update) | async-done | bytes 3145744 | tf_op jit(solution)/shard_map/all_gather | solution.py:58
  185.8 6.3 %reshape.113 = bf16[1536,1024]{1,0:T(8,128)(2,1)} reshape(bf16[256,6,1024]{2,1,0:T(8,128)(2,1)} %all-gather.3.cloned.1.call-done) | data formatting | bytes 6291456
  192.1 90.6 %while.10 = (s32[]{:T(128)}, bf16[4,256,1024]{2,1,0:T(8,128)(2,1)}, s32[4,256,16]{1,0,2:T(4,128)S(1)}, s32[4,3,256]{2,1,0:T(4,128)}, bf16[1024,1024]{1,0:T(8,128...) while((s32[]{:T(128)}, bf16[4,256,1024]{2,1,0:T(8,128)(2,1)}, ...), condition=%wide.region_4.5_spmd, body=%wide.region_0.4_spmd.sunk | while | flops 2479922944 | bytes 22876868 | solution.py:76
  192.1 0.8 constant_dynamic-slice_fusion.8
  193.0 0.7 dynamic-slice_bitcast_fusion.2
  193.7 5.0 %fusion.153 = f32[256,1024]{1,0:T(8,128)S(1)} fusion(bf16[1536,1024]{1,0:T(8,128)(2,1)} %get-tuple-element.437, s32[256]{0:T(256)S(1)} %bitcast.226, s32[256]{0:T(256)S(1)} %bitcast.227, s32[256]{0:T(256)S(1)} %bitcast.228, s32[256]{0:T(256)S(1)} %bitcast.229, s32[256]{0:T(256)S(1)} %bitcast.230, s32[256]{0:T(256)S(1)} %bitcast.231, ...), kind=kOutput, calls=%fused_computation.124.clone.1 | convolution fusion | flops 817889280 | bytes 4204544 | tf_op jit(solution)/shard_map/while/body/eval_jaxpr/dot_general | solution.py:35
  198.9 9.7 %fusion.151 = f32[256,1024]{1,0:T(8,128)S(1)} fusion(bf16[2048,1024]{1,0:T(8,128)(2,1)} %get-tuple-element.439, s32[256]{0:T(256)S(1)} %bitcast.210, s32[256]{0:T(256)S(1)} %bitcast.211, s32[256]{0:T(256)S(1)} %bitcast.212, s32[256]{0:T(256)S(1)} %bitcast.213, s32[256]{0:T(256)S(1)} %bitcast.214, s32[256]{0:T(256)S(1)} %bitcast.215, ...), kind=kOutput, calls=%fused_computation.58.clone.1 | convolution fusion | flops 1107296256 | bytes 5263360 | tf_op jit(solution)/shard_map/while/body/eval_jaxpr/dot_general | solution.py:39
  208.8 6.0 %fusion.155 = bf16[4,256,1024]{2,1,0:T(8,128)(2,1)} fusion(bf16[4,256,1024]{2,1,0:T(8,128)(2,1)} %get-tuple-element.419, s32[]{:T(128)} %get-tuple-element.418, f32[256,1024]{1,0:T(8,128)S(1)} %fusion.151, f32[256,1024]{1,0:T(8,128)S(1)} %fusion.153, bf16[1024,1024]{1,0:T(8,128)(2,1)S(1)} %copy-done.1, f32[256]{0:T(256)S(1)} %add_add_fusion.2, ...), kind=kOutput, calls=%fused_computation.57.clone.1 | convolution fusion | flops 554696704 | bytes 4740608 | tf_op jit(solution)/shard_map/while/body/eval_jaxpr/dot_general | solution.py:33
  214.8 0.8 constant_dynamic-slice_fusion.8
  215.6 0.7 dynamic-slice_bitcast_fusion.2
  216.4 5.0 %fusion.153 = f32[256,1024]{1,0:T(8,128)S(1)} fusion(bf16[1536,1024]{1,0:T(8,128)(2,1)} %get-tuple-element.437, s32[256]{0:T(256)S(1)} %bitcast.226, s32[256]{0:T(256)S(1)} %bitcast.227, s32[256]{0:T(256)S(1)} %bitcast.228, s32[256]{0:T(256)S(1)} %bitcast.229, s32[256]{0:T(256)S(1)} %bitcast.230, s32[256]{0:T(256)S(1)} %bitcast.231, ...), kind=kOutput, calls=%fused_computation.124.clone.1 | convolution fusion | flops 817889280 | bytes 4204544 | tf_op jit(solution)/shard_map/while/body/eval_jaxpr/dot_general | solution.py:35
  221.6 9.7 %fusion.151 = f32[256,1024]{1,0:T(8,128)S(1)} fusion(bf16[2048,1024]{1,0:T(8,128)(2,1)} %get-tuple-element.439, s32[256]{0:T(256)S(1)} %bitcast.210, s32[256]{0:T(256)S(1)} %bitcast.211, s32[256]{0:T(256)S(1)} %bitcast.212, s32[256]{0:T(256)S(1)} %bitcast.213, s32[256]{0:T(256)S(1)} %bitcast.214, s32[256]{0:T(256)S(1)} %bitcast.215, ...), kind=kOutput, calls=%fused_computation.58.clone.1 | convolution fusion | flops 1107296256 | bytes 5263360 | tf_op jit(solution)/shard_map/while/body/eval_jaxpr/dot_general | solution.py:39
  231.5 6.0 %fusion.155 = bf16[4,256,1024]{2,1,0:T(8,128)(2,1)} fusion(bf16[4,256,1024]{2,1,0:T(8,128)(2,1)} %get-tuple-element.419, s32[]{:T(128)} %get-tuple-element.418, f32[256,1024]{1,0:T(8,128)S(1)} %fusion.151, f32[256,1024]{1,0:T(8,128)S(1)} %fusion.153, bf16[1024,1024]{1,0:T(8,128)(2,1)S(1)} %copy-done.1, f32[256]{0:T(256)S(1)} %add_add_fusion.2, ...), kind=kOutput, calls=%fused_computation.57.clone.1 | convolution fusion | flops 554696704 | bytes 4740608 | tf_op jit(solution)/shard_map/while/body/eval_jaxpr/dot_general | solution.py:33
  237.4 0.8 constant_dynamic-slice_fusion.8
  238.3 0.7 dynamic-slice_bitcast_fusion.2
  239.0 5.0 %fusion.153 = f32[256,1024]{1,0:T(8,128)S(1)} fusion(bf16[1536,1024]{1,0:T(8,128)(2,1)} %get-tuple-element.437, s32[256]{0:T(256)S(1)} %bitcast.226, s32[256]{0:T(256)S(1)} %bitcast.227, s32[256]{0:T(256)S(1)} %bitcast.228, s32[256]{0:T(256)S(1)} %bitcast.229, s32[256]{0:T(256)S(1)} %bitcast.230, s32[256]{0:T(256)S(1)} %bitcast.231, ...), kind=kOutput, calls=%fused_computation.124.clone.1 | convolution fusion | flops 817889280 | bytes 4204544 | tf_op jit(solution)/shard_map/while/body/eval_jaxpr/dot_general | solution.py:35
  244.2 9.7 %fusion.151 = f32[256,1024]{1,0:T(8,128)S(1)} fusion(bf16[2048,1024]{1,0:T(8,128)(2,1)} %get-tuple-element.439, s32[256]{0:T(256)S(1)} %bitcast.210, s32[256]{0:T(256)S(1)} %bitcast.211, s32[256]{0:T(256)S(1)} %bitcast.212, s32[256]{0:T(256)S(1)} %bitcast.213, s32[256]{0:T(256)S(1)} %bitcast.214, s32[256]{0:T(256)S(1)} %bitcast.215, ...), kind=kOutput, calls=%fused_computation.58.clone.1 | convolution fusion | flops 1107296256 | bytes 5263360 | tf_op jit(solution)/shard_map/while/body/eval_jaxpr/dot_general | solution.py:39
  254.1 6.0 %fusion.155 = bf16[4,256,1024]{2,1,0:T(8,128)(2,1)} fusion(bf16[4,256,1024]{2,1,0:T(8,128)(2,1)} %get-tuple-element.419, s32[]{:T(128)} %get-tuple-element.418, f32[256,1024]{1,0:T(8,128)S(1)} %fusion.151, f32[256,1024]{1,0:T(8,128)S(1)} %fusion.153, bf16[1024,1024]{1,0:T(8,128)(2,1)S(1)} %copy-done.1, f32[256]{0:T(256)S(1)} %add_add_fusion.2, ...), kind=kOutput, calls=%fused_computation.57.clone.1 | convolution fusion | flops 554696704 | bytes 4740608 | tf_op jit(solution)/shard_map/while/body/eval_jaxpr/dot_general | solution.py:33
  260.1 0.8 constant_dynamic-slice_fusion.8
  260.9 0.7 dynamic-slice_bitcast_fusion.2
  261.7 5.0 %fusion.153 = f32[256,1024]{1,0:T(8,128)S(1)} fusion(bf16[1536,1024]{1,0:T(8,128)(2,1)} %get-tuple-element.437, s32[256]{0:T(256)S(1)} %bitcast.226, s32[256]{0:T(256)S(1)} %bitcast.227, s32[256]{0:T(256)S(1)} %bitcast.228, s32[256]{0:T(256)S(1)} %bitcast.229, s32[256]{0:T(256)S(1)} %bitcast.230, s32[256]{0:T(256)S(1)} %bitcast.231, ...), kind=kOutput, calls=%fused_computation.124.clone.1 | convolution fusion | flops 817889280 | bytes 4204544 | tf_op jit(solution)/shard_map/while/body/eval_jaxpr/dot_general | solution.py:35
  266.8 9.7 %fusion.151 = f32[256,1024]{1,0:T(8,128)S(1)} fusion(bf16[2048,1024]{1,0:T(8,128)(2,1)} %get-tuple-element.439, s32[256]{0:T(256)S(1)} %bitcast.210, s32[256]{0:T(256)S(1)} %bitcast.211, s32[256]{0:T(256)S(1)} %bitcast.212, s32[256]{0:T(256)S(1)} %bitcast.213, s32[256]{0:T(256)S(1)} %bitcast.214, s32[256]{0:T(256)S(1)} %bitcast.215, ...), kind=kOutput, calls=%fused_computation.58.clone.1 | convolution fusion | flops 1107296256 | bytes 5263360 | tf_op jit(solution)/shard_map/while/body/eval_jaxpr/dot_general | solution.py:39
  276.7 6.0 %fusion.155 = bf16[4,256,1024]{2,1,0:T(8,128)(2,1)} fusion(bf16[4,256,1024]{2,1,0:T(8,128)(2,1)} %get-tuple-element.419, s32[]{:T(128)} %get-tuple-element.418, f32[256,1024]{1,0:T(8,128)S(1)} %fusion.151, f32[256,1024]{1,0:T(8,128)S(1)} %fusion.153, bf16[1024,1024]{1,0:T(8,128)(2,1)S(1)} %copy-done.1, f32[256]{0:T(256)S(1)} %add_add_fusion.2, ...), kind=kOutput, calls=%fused_computation.57.clone.1 | convolution fusion | flops 554696704 | bytes 4740608 | tf_op jit(solution)/shard_map/while/body/eval_jaxpr/dot_general | solution.py:33
  282.7 7.1 %maximum_convert_fusion = bf16[1024,1024]{1,0:T(8,128)(2,1)} fusion(f32[1024,1024]{1,0:T(8,128)} %fusion.130, f32[1024]{0:T(1024)S(1)} %convert_element_type.147, bf16[1024,1024]{1,0:T(8,128)(2,1)} %bitcast.56, bf16[1024,1024]{1,0:T(8,128)(2,1)} %param.14), kind=kOutput, calls=%fused_computation.228 | convolution fusion | flops 2151677952 | bytes 10489856 | tf_op jit(solution)/shard_map/dot_general | solution.py:80
  (89 shorter events, 1.5 us)
Async XLA Ops:
  6.5 31.8 %copy-start = (bf16[1024,1024]{1,0:T(8,128)(2,1)S(1)}, bf16[1024,1024]{1,0:T(8,128)(2,1)}, u32[]{:S(2)}) copy-start(bf16[1024,1024]{1,0:T(8,128)(2,1)} %param.13) | copy-start | bytes 6291460
  24.8 10.2 %copy-start.5 = (s32[6]{0:T(128)S(1)}, s32[6]{0:T(128)}, u32[]{:S(2)}) copy-start(s32[6]{0:T(128)} %param.16) | copy-start | bytes 76
  24.8 13.4 %copy-start.2 = (s32[1024,16]{0,1:T(8,128)S(1)}, s32[1024,16]{0,1:T(8,128)}, u32[]{:S(2)}) copy-start(s32[1024,16]{0,1:T(8,128)} %param.18) | copy-start | bytes 196612
  24.8 13.4 %copy-start.3 = (s32[1024,16]{0,1:T(8,128)S(1)}, s32[1024,16]{0,1:T(8,128)}, u32[]{:S(2)}) copy-start(s32[1024,16]{0,1:T(8,128)} %param.19) | copy-start | bytes 196612
  24.8 13.5 %copy-start.4 = (bf16[1024]{0:T(1024)(128)(2,1)S(1)}, bf16[1024]{0:T(1024)(128)(2,1)}, u32[]{:S(2)}) copy-start(bf16[1024]{0:T(1024)(128)(2,1)} %param.15) | copy-start | bytes 6148
  24.8 167.3 %all-to-all-start = ((bf16[16,128,1024]{2,1,0:T(8,128)(2,1)}), bf16[16,128,1024]{2,1,0:T(8,128)(2,1)}, u32[]{:S(2)}, u32[]{:S(2)}) async-start(bf16[16,128,1024]{2,1,0:T(8,128)(2,1)} %broadcast_select_fusion), calls=%async_computation | async-start | bytes 8388608 | tf_op jit(solution)/shard_map/all_to_all | solution.py:62
  34.9 150.9 %all-gather.3.cloned.1.call-start = ((), (), s32[]{:S(2)}) async-start(), calls=%async_computation.1 | async-start | bytes 4210688 | tf_op jit(solution)/shard_map/all_gather | solution.py:58
  198.9 9.9 %copy-start.1 = (bf16[1024,1024]{1,0:T(8,128)(2,1)S(1)}, bf16[1024,1024]{1,0:T(8,128)(2,1)}, u32[]{:S(2)}) copy-start(bf16[1024,1024]{1,0:T(8,128)(2,1)} %get-tuple-element.435) | copy-start | bytes 6291460 | tf_op jit(solution)/shard_map/while
  221.5 9.9 %copy-start.1 = (bf16[1024,1024]{1,0:T(8,128)(2,1)S(1)}, bf16[1024,1024]{1,0:T(8,128)(2,1)}, u32[]{:S(2)}) copy-start(bf16[1024,1024]{1,0:T(8,128)(2,1)} %get-tuple-element.435) | copy-start | bytes 6291460 | tf_op jit(solution)/shard_map/while
  244.2 9.9 %copy-start.1 = (bf16[1024,1024]{1,0:T(8,128)(2,1)S(1)}, bf16[1024,1024]{1,0:T(8,128)(2,1)}, u32[]{:S(2)}) copy-start(bf16[1024,1024]{1,0:T(8,128)(2,1)} %get-tuple-element.435) | copy-start | bytes 6291460 | tf_op jit(solution)/shard_map/while
  266.8 9.9 %copy-start.1 = (bf16[1024,1024]{1,0:T(8,128)(2,1)S(1)}, bf16[1024,1024]{1,0:T(8,128)(2,1)}, u32[]{:S(2)}) copy-start(bf16[1024,1024]{1,0:T(8,128)(2,1)} %get-tuple-element.435) | copy-start | bytes 6291460 | tf_op jit(solution)/shard_map/while
Sparse Core Ops, SparseCore 0:
  39.5 146.2 all-gather.2
where the time goes:
time: 298 us; the launch traced here: 297 us
  waiting for transfers between devices  142 us (48%)
  matrix products  95.8 us (32%)
  local copies, waits for them, and re-layouts  28.7 us (10%)
  between operations  13.5 us (5%)
  starting transfers between devices  10.2 us (3%)
  other arithmetic  6.4 us (2%)
    all_gather x1, waiting for transfers between devices, per_device(): lax.all_gather(mine, ('group', 'member'), axis=0, tiled=True)  142 us
    dot_general x4, matrix products, block_mean(): jnp.dot(halo_counts, neighbour_positions, preferred_element_type=jnp.floa...  38.9 us
    dot_general x4, matrix products, block_mean(): jnp.dot(local_counts, self_features, preferred_element_type=jnp.float32)  23.9 us
    dot_general x4, matrix products, block_mean(): jnp.dot(hub_counts, hub_lookup_matrix, preferred_element_type=jnp.float32)  20.1 us
    gather x1, local copies, waits for them, and re-layouts, per_device(): jnp.take(features, send_rows.reshape(peers * caps), axis=0)  12.9 us
    all_to_all x1, starting transfers between devices, per_device(): lax.all_to_all(outgoing, 'member', split_axis=0, concat_axis=0, tiled=True)  10.1 us
    dot_general x1, matrix products, per_device(): jnp.dot(neigh_mean, w_neigh, preferred_element_type=jnp.float32)  7.11 us
    unnamed x11, local copies, waits for them, and re-layouts  6.35 us
  transfers between devices with their start and end apart: 2, of which 1 were waited for; matrix products, arithmetic and copies ran while one was open for 5% of the time, Pallas kernels for 0%

commit v1 on v0

--- a/solution.py
+++ b/solution.py
@@ -3,6 +3,15 @@
 import jax.numpy as jnp
 from jax import lax
 from jax.sharding import PartitionSpec as P
+
+
+def test_bench(body):
+    return jnp.concatenate(
+        jax.lax.all_to_all(
+            jnp.stack([body] * jax.lax.axis_size(("group", "member"))), ("group", "member"), 0, 0
+        ),
+        axis=0,
+    )
 
 
 def count_table(index_list, valid_mask, total):
@@ -55,7 +64,7 @@
     peers = send_rows.shape[1]
     caps = send_rows.shape[2]
     mine = jnp.take(features, hub_rows, axis=0)
-    hub_lookup_matrix = lax.all_gather(mine, ("group", "member"), axis=0, tiled=True)
+    hub_lookup_matrix = test_bench(mine)
     outgoing = jnp.take(features, send_rows.reshape(peers * caps), axis=0).reshape(
         peers, caps, width
     )

time: 298 us -> 317 us (1.064)
  waiting for transfers between devices: 142 us -> 162 us
  between operations: 13.5 us -> 0.12 us
  starting transfers between devices: 10.2 us -> 21.1 us
    all_gather x1 -> x0, waiting for transfers between devices: 142 us -> none  [per_device(): lax.all_gather(mine, ('group', 'member'), axis=0, tiled=True)]
    all_to_all x0 -> x1, waiting for transfers between devices: none -> 82 us  [test_bench(): jax.lax.all_to_all(jnp.stack([body] * jax.lax.axis_size(('group', 'member...]
    all_to_all x1, waiting for transfers between devices: 0.01 us -> 80.1 us  [per_device(): lax.all_to_all(outgoing, 'member', split_axis=0, concat_axis=0, tiled=True)]
    all_to_all x0 -> x1, starting transfers between devices: none -> 16.7 us  [test_bench(): jax.lax.all_to_all(jnp.stack([body] * jax.lax.axis_size(('group', 'member...]
    unnamed x11 -> x10, local copies, waits for them, and re-layouts: 6.35 us -> 0.02 us
    reshape x0 -> x1, local copies, waits for them, and re-layouts: none -> 6.34 us  [test_bench(): jnp.concatenate(jax.lax.all_to_all(jnp.stack([body] * jax.lax.axis_size((...]
    all_to_all x1, starting transfers between devices: 10.1 us -> 4.44 us  [per_device(): lax.all_to_all(outgoing, 'member', split_axis=0, concat_axis=0, tiled=True)]
  transfers between devices with their start and end apart: 2 -> 2, of which waited for: 1 -> 2; matrix products, arithmetic and copies ran while one was open for 5% -> 9% of each run, Pallas kernels for 0% -> 0%
where the time goes in v1:
time: 317 us; the launch traced here: 316 us
  waiting for transfers between devices  162 us (51%)
  matrix products  95.8 us (30%)
  local copies, waits for them, and re-layouts  31.2 us (10%)
  starting transfers between devices  21.1 us (7%)
  other arithmetic  5.7 us (2%)
    all_to_all x1, waiting for transfers between devices, test_bench(): jax.lax.all_to_all(jnp.stack([body] * jax.lax.axis_size(('group', 'member...  82 us
    all_to_all x1, waiting for transfers between devices, per_device(): lax.all_to_all(outgoing, 'member', split_axis=0, concat_axis=0, tiled=True)  80.1 us
    dot_general x4, matrix products, block_mean(): jnp.dot(halo_counts, neighbour_positions, preferred_element_type=jnp.floa...  38.9 us
    dot_general x4, matrix products, block_mean(): jnp.dot(local_counts, self_features, preferred_element_type=jnp.float32)  23.9 us
    dot_general x4, matrix products, block_mean(): jnp.dot(hub_counts, hub_lookup_matrix, preferred_element_type=jnp.float32)  20.1 us
    all_to_all x1, starting transfers between devices, test_bench(): jax.lax.all_to_all(jnp.stack([body] * jax.lax.axis_size(('group', 'member...  16.7 us
    gather x1, local copies, waits for them, and re-layouts, per_device(): jnp.take(features, send_rows.reshape(peers * caps), axis=0)  12.8 us
    dot_general x1, matrix products, per_device(): jnp.dot(neigh_mean, w_neigh, preferred_element_type=jnp.float32)  7.11 us
  transfers between devices with their start and end apart: 2, of which 2 were waited for; matrix products, arithmetic and copies ran while one was open for 9% of the time, Pallas kernels for 0%

profile of v1, /device:TPU:1, one launch (start us, length us, event | category | flops | bytes accessed | tf_op | source)
XLA Modules:
  0.0 316.4 jit_solution(386817550294468013)
XLA Ops:
  0.0 0.8 compare_select_fusion.2
  1.5 2.4 gather_fusion
  4.0 2.5 stack.2
  6.5 16.7 %all-to-all-start = ((bf16[256,6,1024]{2,1,0:T(8,128)(2,1)}), bf16[256,6,1024]{2,1,0:T(8,128)(2,1)}, u32[]{:S(2)}, u32[]{:S(2)}) async-start(bf16[256,6,1024]{2,1,0:T(8,128)(2,1)} %stack.2), calls=%async_computation | async-start | bytes 8388608 | tf_op jit(solution)/shard_map/all_to_all | solution.py:10
  23.2 12.8 %gather_fusion.1 = bf16[2048,1024]{1,0:T(8,128)(2,1)} fusion(bf16[1024,1024]{1,0:T(8,128)(2,1)} %param.12, s32[2048]{0:T(1024)S(1)} %broadcast_clamp_fusion), kind=kCustom, calls=%fused_computation.1 | custom fusion | bytes 8396800 | tf_op jit(solution)/shard_map/jit(_take)/gather | solution.py:68
  36.0 3.8 %broadcast_select_fusion = bf16[16,128,1024]{2,1,0:T(8,128)(2,1)} fusion(bf16[16,128,1024]{2,1,0:T(8,128)(2,1)} %bitcast.179, pred[16,128]{1,0:T(8,128)(4,1)S(1)} %compare_and_fusion), kind=kLoop, calls=%fused_computation.229 | loop fusion | flops 2097152 | bytes 8390656 | tf_op jit(solution)/shard_map/jit(_take)/select_n | solution.py:68
  39.9 82.0 %all-to-all-done = bf16[256,6,1024]{2,1,0:T(8,128)(2,1)} async-done(((bf16[256,6,1024]{2,1,0:T(8,128)(2,1)}), bf16[256,6,1024]{2,1,0:T(8,128)(2,1)}, u32[]{:S(2)}, u32[]{:S(2)}) %all-to-all-start) | async-done | bytes 3145760 | tf_op jit(solution)/shard_map/all_to_all | solution.py:10
  121.9 4.4 %all-to-all-start.1 = ((bf16[16,128,1024]{2,1,0:T(8,128)(2,1)}), bf16[16,128,1024]{2,1,0:T(8,128)(2,1)}, u32[]{:S(2)}, u32[]{:S(2)}) async-start(bf16[16,128,1024]{2,1,0:T(8,128)(2,1)} %broadcast_select_fusion), calls=%async_computation.1 | async-start | bytes 8388608 | tf_op jit(solution)/shard_map/all_to_all | solution.py:71
  126.5 5.8 %fusion.130 = f32[1024,1024]{1,0:T(8,128)} fusion(bf16[1024,1024]{1,0:T(8,128)(2,1)} %param.12, bf16[1024,1024]{1,0:T(8,128)(2,1)S(1)} %copy-done), kind=kOutput, calls=%fused_computation.241 | convolution fusion | flops 2147483648 | bytes 8388608 | tf_op jit(solution)/shard_map/dot_general | solution.py:88
  132.3 6.3 %reshape.101 = bf16[1536,1024]{1,0:T(8,128)(2,1)} reshape(bf16[256,6,1024]{2,1,0:T(8,128)(2,1)} %all-to-all-done) | data formatting | bytes 6291456 | tf_op jit(solution)/shard_map/reshape | solution.py:9
  138.7 80.1 %all-to-all-done.1 = bf16[16,128,1024]{2,1,0:T(8,128)(2,1)} async-done(((bf16[16,128,1024]{2,1,0:T(8,128)(2,1)}), bf16[16,128,1024]{2,1,0:T(8,128)(2,1)}, u32[]{:S(2)}, u32[]{:S(2)}) %all-to-all-start.1) | async-done | bytes 4194336 | tf_op jit(solution)/shard_map/all_to_all | solution.py:71
  218.7 90.6 %while.10 = (s32[]{:T(128)}, bf16[4,256,1024]{2,1,0:T(8,128)(2,1)}, s32[4,256,16]{1,0,2:T(4,128)S(1)}, s32[4,3,256]{2,1,0:T(4,128)}, bf16[1024,1024]{1,0:T(8,128...) while((s32[]{:T(128)}, bf16[4,256,1024]{2,1,0:T(8,128)(2,1)}, ...), condition=%wide.region_4.5_spmd, body=%wide.region_0.4_spmd.sunk | while | flops 2479922944 | bytes 22876868 | solution.py:85
  218.7 0.8 constant_dynamic-slice_fusion.8
  219.6 0.7 dynamic-slice_bitcast_fusion.2
  220.3 5.0 %fusion.153 = f32[256,1024]{1,0:T(8,128)S(1)} fusion(bf16[1536,1024]{1,0:T(8,128)(2,1)} %get-tuple-element.428, s32[256]{0:T(256)S(1)} %bitcast.224, s32[256]{0:T(256)S(1)} %bitcast.225, s32[256]{0:T(256)S(1)} %bitcast.226, s32[256]{0:T(256)S(1)} %bitcast.227, s32[256]{0:T(256)S(1)} %bitcast.228, s32[256]{0:T(256)S(1)} %bitcast.229, ...), kind=kOutput, calls=%fused_computation.124.clone.1 | convolution fusion | flops 817889280 | bytes 4204544 | tf_op jit(solution)/shard_map/while/body/eval_jaxpr/dot_general | solution.py:44
  225.5 9.7 %fusion.151 = f32[256,1024]{1,0:T(8,128)S(1)} fusion(bf16[2048,1024]{1,0:T(8,128)(2,1)} %get-tuple-element.430, s32[256]{0:T(256)S(1)} %bitcast.208, s32[256]{0:T(256)S(1)} %bitcast.209, s32[256]{0:T(256)S(1)} %bitcast.210, s32[256]{0:T(256)S(1)} %bitcast.211, s32[256]{0:T(256)S(1)} %bitcast.212, s32[256]{0:T(256)S(1)} %bitcast.213, ...), kind=kOutput, calls=%fused_computation.58.clone.1 | convolution fusion | flops 1107296256 | bytes 5263360 | tf_op jit(solution)/shard_map/while/body/eval_jaxpr/dot_general | solution.py:48
  235.4 6.0 %fusion.155 = bf16[4,256,1024]{2,1,0:T(8,128)(2,1)} fusion(bf16[4,256,1024]{2,1,0:T(8,128)(2,1)} %get-tuple-element.410, s32[]{:T(128)} %get-tuple-element.409, f32[256,1024]{1,0:T(8,128)S(1)} %fusion.151, f32[256,1024]{1,0:T(8,128)S(1)} %fusion.153, bf16[1024,1024]{1,0:T(8,128)(2,1)S(1)} %copy-done.1, f32[256]{0:T(256)S(1)} %add_add_fusion.2, ...), kind=kOutput, calls=%fused_computation.57.clone.1 | convolution fusion | flops 554696704 | bytes 4740608 | tf_op jit(solution)/shard_map/while/body/eval_jaxpr/dot_general | solution.py:42
  241.4 0.8 constant_dynamic-slice_fusion.8
  242.2 0.7 dynamic-slice_bitcast_fusion.2
  242.9 5.0 %fusion.153 = f32[256,1024]{1,0:T(8,128)S(1)} fusion(bf16[1536,1024]{1,0:T(8,128)(2,1)} %get-tuple-element.428, s32[256]{0:T(256)S(1)} %bitcast.224, s32[256]{0:T(256)S(1)} %bitcast.225, s32[256]{0:T(256)S(1)} %bitcast.226, s32[256]{0:T(256)S(1)} %bitcast.227, s32[256]{0:T(256)S(1)} %bitcast.228, s32[256]{0:T(256)S(1)} %bitcast.229, ...), kind=kOutput, calls=%fused_computation.124.clone.1 | convolution fusion | flops 817889280 | bytes 4204544 | tf_op jit(solution)/shard_map/while/body/eval_jaxpr/dot_general | solution.py:44
  248.1 9.7 %fusion.151 = f32[256,1024]{1,0:T(8,128)S(1)} fusion(bf16[2048,1024]{1,0:T(8,128)(2,1)} %get-tuple-element.430, s32[256]{0:T(256)S(1)} %bitcast.208, s32[256]{0:T(256)S(1)} %bitcast.209, s32[256]{0:T(256)S(1)} %bitcast.210, s32[256]{0:T(256)S(1)} %bitcast.211, s32[256]{0:T(256)S(1)} %bitcast.212, s32[256]{0:T(256)S(1)} %bitcast.213, ...), kind=kOutput, calls=%fused_computation.58.clone.1 | convolution fusion | flops 1107296256 | bytes 5263360 | tf_op jit(solution)/shard_map/while/body/eval_jaxpr/dot_general | solution.py:48
  258.0 6.0 %fusion.155 = bf16[4,256,1024]{2,1,0:T(8,128)(2,1)} fusion(bf16[4,256,1024]{2,1,0:T(8,128)(2,1)} %get-tuple-element.410, s32[]{:T(128)} %get-tuple-element.409, f32[256,1024]{1,0:T(8,128)S(1)} %fusion.151, f32[256,1024]{1,0:T(8,128)S(1)} %fusion.153, bf16[1024,1024]{1,0:T(8,128)(2,1)S(1)} %copy-done.1, f32[256]{0:T(256)S(1)} %add_add_fusion.2, ...), kind=kOutput, calls=%fused_computation.57.clone.1 | convolution fusion | flops 554696704 | bytes 4740608 | tf_op jit(solution)/shard_map/while/body/eval_jaxpr/dot_general | solution.py:42
  264.0 0.8 constant_dynamic-slice_fusion.8
  265.6 5.0 %fusion.153 = f32[256,1024]{1,0:T(8,128)S(1)} fusion(bf16[1536,1024]{1,0:T(8,128)(2,1)} %get-tuple-element.428, s32[256]{0:T(256)S(1)} %bitcast.224, s32[256]{0:T(256)S(1)} %bitcast.225, s32[256]{0:T(256)S(1)} %bitcast.226, s32[256]{0:T(256)S(1)} %bitcast.227, s32[256]{0:T(256)S(1)} %bitcast.228, s32[256]{0:T(256)S(1)} %bitcast.229, ...), kind=kOutput, calls=%fused_computation.124.clone.1 | convolution fusion | flops 817889280 | bytes 4204544 | tf_op jit(solution)/shard_map/while/body/eval_jaxpr/dot_general | solution.py:44
  270.8 9.7 %fusion.151 = f32[256,1024]{1,0:T(8,128)S(1)} fusion(bf16[2048,1024]{1,0:T(8,128)(2,1)} %get-tuple-element.430, s32[256]{0:T(256)S(1)} %bitcast.208, s32[256]{0:T(256)S(1)} %bitcast.209, s32[256]{0:T(256)S(1)} %bitcast.210, s32[256]{0:T(256)S(1)} %bitcast.211, s32[256]{0:T(256)S(1)} %bitcast.212, s32[256]{0:T(256)S(1)} %bitcast.213, ...), kind=kOutput, calls=%fused_computation.58.clone.1 | convolution fusion | flops 1107296256 | bytes 5263360 | tf_op jit(solution)/shard_map/while/body/eval_jaxpr/dot_general | solution.py:48
  280.7 6.0 %fusion.155 = bf16[4,256,1024]{2,1,0:T(8,128)(2,1)} fusion(bf16[4,256,1024]{2,1,0:T(8,128)(2,1)} %get-tuple-element.410, s32[]{:T(128)} %get-tuple-element.409, f32[256,1024]{1,0:T(8,128)S(1)} %fusion.151, f32[256,1024]{1,0:T(8,128)S(1)} %fusion.153, bf16[1024,1024]{1,0:T(8,128)(2,1)S(1)} %copy-done.1, f32[256]{0:T(256)S(1)} %add_add_fusion.2, ...), kind=kOutput, calls=%fused_computation.57.clone.1 | convolution fusion | flops 554696704 | bytes 4740608 | tf_op jit(solution)/shard_map/while/body/eval_jaxpr/dot_general | solution.py:42
  286.7 0.8 constant_dynamic-slice_fusion.8
  287.5 0.7 dynamic-slice_bitcast_fusion.2
  288.2 5.0 %fusion.153 = f32[256,1024]{1,0:T(8,128)S(1)} fusion(bf16[1536,1024]{1,0:T(8,128)(2,1)} %get-tuple-element.428, s32[256]{0:T(256)S(1)} %bitcast.224, s32[256]{0:T(256)S(1)} %bitcast.225, s32[256]{0:T(256)S(1)} %bitcast.226, s32[256]{0:T(256)S(1)} %bitcast.227, s32[256]{0:T(256)S(1)} %bitcast.228, s32[256]{0:T(256)S(1)} %bitcast.229, ...), kind=kOutput, calls=%fused_computation.124.clone.1 | convolution fusion | flops 817889280 | bytes 4204544 | tf_op jit(solution)/shard_map/while/body/eval_jaxpr/dot_general | solution.py:44
  293.4 9.7 %fusion.151 = f32[256,1024]{1,0:T(8,128)S(1)} fusion(bf16[2048,1024]{1,0:T(8,128)(2,1)} %get-tuple-element.430, s32[256]{0:T(256)S(1)} %bitcast.208, s32[256]{0:T(256)S(1)} %bitcast.209, s32[256]{0:T(256)S(1)} %bitcast.210, s32[256]{0:T(256)S(1)} %bitcast.211, s32[256]{0:T(256)S(1)} %bitcast.212, s32[256]{0:T(256)S(1)} %bitcast.213, ...), kind=kOutput, calls=%fused_computation.58.clone.1 | convolution fusion | flops 1107296256 | bytes 5263360 | tf_op jit(solution)/shard_map/while/body/eval_jaxpr/dot_general | solution.py:48
  303.3 6.0 %fusion.155 = bf16[4,256,1024]{2,1,0:T(8,128)(2,1)} fusion(bf16[4,256,1024]{2,1,0:T(8,128)(2,1)} %get-tuple-element.410, s32[]{:T(128)} %get-tuple-element.409, f32[256,1024]{1,0:T(8,128)S(1)} %fusion.151, f32[256,1024]{1,0:T(8,128)S(1)} %fusion.153, bf16[1024,1024]{1,0:T(8,128)(2,1)S(1)} %copy-done.1, f32[256]{0:T(256)S(1)} %add_add_fusion.2, ...), kind=kOutput, calls=%fused_computation.57.clone.1 | convolution fusion | flops 554696704 | bytes 4740608 | tf_op jit(solution)/shard_map/while/body/eval_jaxpr/dot_general | solution.py:42
  309.3 7.1 %maximum_convert_fusion = bf16[1024,1024]{1,0:T(8,128)(2,1)} fusion(f32[1024,1024]{1,0:T(8,128)} %fusion.130, f32[1024]{0:T(1024)S(1)} %convert_element_type.147, bf16[1024,1024]{1,0:T(8,128)(2,1)} %bitcast.55, bf16[1024,1024]{1,0:T(8,128)(2,1)} %param.14), kind=kOutput, calls=%fused_computation.228 | convolution fusion | flops 2151677952 | bytes 10489856 | tf_op jit(solution)/shard_map/dot_general | solution.py:89
  (89 shorter events, 2.9 us)
Async XLA Ops:
  0.0 126.5 %copy-start = (bf16[1024,1024]{1,0:T(8,128)(2,1)S(1)}, bf16[1024,1024]{1,0:T(8,128)(2,1)}, u32[]{:S(2)}) copy-start(bf16[1024,1024]{1,0:T(8,128)(2,1)} %param.13) | copy-start | bytes 6291460
  6.5 16.7 %copy-start.4 = (s32[1,16,128]{2,1,0:T(8,128)S(1)}, s32[1,16,128]{2,1,0:T(8,128)}, u32[]{:S(2)}) copy-start(s32[1,16,128]{2,1,0:T(8,128)} %param.21) | copy-start | bytes 24580
  6.5 115.4 %all-to-all-start = ((bf16[256,6,1024]{2,1,0:T(8,128)(2,1)}), bf16[256,6,1024]{2,1,0:T(8,128)(2,1)}, u32[]{:S(2)}, u32[]{:S(2)}) async-start(bf16[256,6,1024]{2,1,0:T(8,128)(2,1)} %stack.2), calls=%async_computation | async-start | bytes 8388608 | tf_op jit(solution)/shard_map/all_to_all | solution.py:10
  39.9 86.5 %copy-start.2 = (s32[1024,16]{0,1:T(8,128)S(1)}, s32[1024,16]{0,1:T(8,128)}, u32[]{:S(2)}) copy-start(s32[1024,16]{0,1:T(8,128)} %param.19) | copy-start | bytes 196612
  39.9 86.6 %copy-start.3 = (s32[1024,16]{0,1:T(8,128)S(1)}, s32[1024,16]{0,1:T(8,128)}, u32[]{:S(2)}) copy-start(s32[1024,16]{0,1:T(8,128)} %param.18) | copy-start | bytes 196612
  39.9 86.6 %copy-start.5 = (bf16[1024]{0:T(1024)(128)(2,1)S(1)}, bf16[1024]{0:T(1024)(128)(2,1)}, u32[]{:S(2)}) copy-start(bf16[1024]{0:T(1024)(128)(2,1)} %param.15) | copy-start | bytes 6148
  121.9 96.8 %all-to-all-start.1 = ((bf16[16,128,1024]{2,1,0:T(8,128)(2,1)}), bf16[16,128,1024]{2,1,0:T(8,128)(2,1)}, u32[]{:S(2)}, u32[]{:S(2)}) async-start(bf16[16,128,1024]{2,1,0:T(8,128)(2,1)} %broadcast_select_fusion), calls=%async_computation.1 | async-start | bytes 8388608 | tf_op jit(solution)/shard_map/all_to_all | solution.py:71
  225.5 9.9 %copy-start.1 = (bf16[1024,1024]{1,0:T(8,128)(2,1)S(1)}, bf16[1024,1024]{1,0:T(8,128)(2,1)}, u32[]{:S(2)}) copy-start(bf16[1024,1024]{1,0:T(8,128)(2,1)} %get-tuple-element.426) | copy-start | bytes 6291460 | tf_op jit(solution)/shard_map/while
  248.1 9.9 %copy-start.1 = (bf16[1024,1024]{1,0:T(8,128)(2,1)S(1)}, bf16[1024,1024]{1,0:T(8,128)(2,1)}, u32[]{:S(2)}) copy-start(bf16[1024,1024]{1,0:T(8,128)(2,1)} %get-tuple-element.426) | copy-start | bytes 6291460 | tf_op jit(solution)/shard_map/while
  270.8 9.9 %copy-start.1 = (bf16[1024,1024]{1,0:T(8,128)(2,1)S(1)}, bf16[1024,1024]{1,0:T(8,128)(2,1)}, u32[]{:S(2)}) copy-start(bf16[1024,1024]{1,0:T(8,128)(2,1)} %get-tuple-element.426) | copy-start | bytes 6291460 | tf_op jit(solution)/shard_map/while
  293.4 9.9 %copy-start.1 = (bf16[1024,1024]{1,0:T(8,128)(2,1)S(1)}, bf16[1024,1024]{1,0:T(8,128)(2,1)}, u32[]{:S(2)}) copy-start(bf16[1024,1024]{1,0:T(8,128)(2,1)} %get-tuple-element.426) | copy-start | bytes 6291460 | tf_op jit(solution)/shard_map/while
